TPU v7x, 256 devices: a whole 4x4x8 slice. The times are simulated.
256 devices in a mesh: expert: 16 (over y, x), tensor: 16 (over z, core).
Axes of the slice: x: 4, y: 4, z: 8, core: 2. Of those that a mesh axis runs over, the one named last changes fastest.
Arguments:
- queries: bfloat16 [4096, 8192], P('expert', 'tensor'), may hold values from -8 to 8
- keys_values: bfloat16 [16, 4, 1280, 256], P('expert'), may hold values from -6 to 6
- prefix_len: int32 [16], P('expert'), may hold values from 128 to 1024, as said below
- out_proj: bfloat16 [8192, 4096], P('tensor', 'expert'), may hold values from -0.0625 to 0.0625
- residual: bfloat16 [4096, 4096], P(('expert', 'tensor')), may hold values from -1.796875 to 1.796875
- norm_gain: float32 [4096], replicated, may hold values from 0.1 to 1.9
- expert_ids: int32 [4096, 8], P('expert'), may hold values from 0 to 63, all different within a row; in each aligned block of 16 rows (0 to 15, 16 to 31, ...) at most 3 rows name the same one
- route_weights: bfloat16 [4096, 8], P('expert'), may hold values from 0.19921875 to 1
- w_gate: bfloat16 [256, 4096, 384], P(('expert', 'tensor')), may hold values from -0.09375 to 0.09375
- w_up: bfloat16 [256, 4096, 384], P(('expert', 'tensor')), may hold values from -0.09375 to 0.09375
- w_down: bfloat16 [256, 384, 4096], P(('expert', 'tensor')), may hold values from -0.15625 to 0.15625
Outputs:
- layer_out: bfloat16 [4096, 4096], P(('expert', 'tensor'))
Inputs may be any that keep to these rules, and one draw needn't show every extreme that they name: `expert_ids`: in the rows of one device (aligned blocks of 16 rows) no expert is named by more than 3 rows, a bound that some block reaches; a row names 8 different experts. `prefix_len`: some sequence has all 1024 slots live.
All inputs are finite; a program needn't handle non-finite values.
Results may differ from a plain program's by a relative error of at most 0.035.
Values may be sent and summed in bfloat16 or wider, within the bound.
No kernel may reach another device: no remote copies, remote signals or barrier semaphores. Data moves between devices by JAX's collectives and lax.ppermute only.
A program may use at most 128 MiB of HBM per device.

v0:
```python
import math
import jax
import jax.numpy as jnp
from jax import lax
from jax.sharding import PartitionSpec as P

HEADS = 64
KVH = 4
HD = 128
TOPK = 8
HSPLIT = 4
TOK_DEV = 16
PREFIX = 1024


def norm_rows(hidden_state, norm_gain):
    values = hidden_state.astype(jnp.float32)
    factor = lax.rsqrt(jnp.mean(values * values, axis=-1, keepdims=True) + 1e-06)
    return (values * factor * norm_gain[None, :]).astype(jnp.bfloat16)


def route_tables(expert_ids, route_weights, experts, most_rows):
    total_rows = expert_ids.shape[0]
    named_mask = expert_ids[:, :, None] == jnp.arange(experts, dtype=jnp.int32)[None, None, :]
    hit_table = jnp.sum(named_mask.astype(jnp.int32), axis=1)
    weight_table = jnp.sum(
        jnp.where(named_mask, route_weights[:, :, None].astype(jnp.float32), 0.0), axis=1
    )
    grouped = hit_table.reshape(total_rows // TOK_DEV, TOK_DEV, experts)
    rank_table = (jnp.cumsum(grouped, axis=1) - grouped).reshape(total_rows, experts)
    share_index = (jnp.arange(total_rows, dtype=jnp.int32) // TOK_DEV)[:, None]
    position_table = share_index * most_rows + rank_table
    return (hit_table, weight_table, rank_table, position_table)


def pick_slot(table, expert_count, slot_count, slot_index):
    shaped = table.reshape(table.shape[0], expert_count, slot_count)
    return lax.dynamic_index_in_dim(shaped, slot_index, 2, keepdims=False)


def shards(
    queries,
    keys_values,
    prefix_len,
    out_proj,
    residual,
    norm_gain,
    expert_ids,
    route_weights,
    w_gate,
    w_up,
    w_down,
):
    tensor_count = lax.axis_size("tensor")
    expert_count = lax.axis_size("expert")
    tensor_index = lax.axis_index("tensor")
    step_rows = queries.shape[0]
    per_device = queries.shape[1] // HD
    group_size = HEADS // KVH
    kv_index = tensor_index * per_device // group_size
    cached = lax.dynamic_index_in_dim(keys_values[0], kv_index, 0, keepdims=False)
    key_rows = cached[:, :HD]
    value_rows = cached[:, HD:]
    context = cached.shape[0]
    query_rows = queries.reshape(step_rows, per_device, HD)
    scores = jnp.einsum(
        "nhd,cd->hnc", query_rows, key_rows, preferred_element_type=jnp.float32
    ) / math.sqrt(HD)
    columns = jnp.arange(context, dtype=jnp.int32)[None, :]
    positions = jnp.arange(step_rows, dtype=jnp.int32)[:, None]
    visible = ((columns < prefix_len[0]) | (columns >= PREFIX) & (columns - PREFIX <= positions))[
        None
    ]
    highest = jnp.max(jnp.where(visible, scores, -1e30), axis=-1, keepdims=True)
    weights = jnp.exp(jnp.where(visible, scores - highest, -1e30))
    summed = jnp.sum(weights, axis=-1)
    blended = jnp.einsum(
        "hnc,cd->nhd", weights.astype(jnp.bfloat16), value_rows, preferred_element_type=jnp.float32
    )
    attended = (
        (blended / jnp.transpose(summed)[:, :, None])
        .astype(jnp.bfloat16)
        .reshape(step_rows, per_device * HD)
    )
    head_part = jnp.dot(
        attended,
        lax.all_gather(out_proj, "expert", axis=1, tiled=True),
        preferred_element_type=jnp.float32,
    )
    slot_count = tensor_count // HSPLIT
    experts = expert_count * slot_count
    most_rows = min(TOK_DEV, max(2, TOK_DEV * TOPK // experts + 1))
    capacity = tensor_count * most_rows
    slot_index = tensor_index // HSPLIT
    start_row = tensor_index * TOK_DEV
    hit_table, weight_table, rank_table, position_table = route_tables(
        expert_ids, route_weights, experts, most_rows
    )
    hit_slot = pick_slot(hit_table, expert_count, slot_count, slot_index)
    weight_slot = pick_slot(weight_table, expert_count, slot_count, slot_index)
    position_slot = pick_slot(position_table, expert_count, slot_count, slot_index)
    slot_match = (hit_slot[:, :, None] == 1) & (
        position_slot[:, :, None] == jnp.arange(capacity, dtype=jnp.int32)[None, None, :]
    )
    head_sum = lax.psum(head_part.astype(jnp.bfloat16), "tensor").astype(jnp.float32)
    residual_full = lax.all_gather(residual, "tensor", axis=0, tiled=True)
    state_full = (residual_full.astype(jnp.float32) + head_sum).astype(jnp.bfloat16)
    hidden_state = lax.dynamic_slice_in_dim(state_full, start_row, TOK_DEV, 0)
    normed_full = norm_rows(state_full, norm_gain)
    source_rows = jnp.sum(
        jnp.where(slot_match, jnp.arange(step_rows, dtype=jnp.int32)[:, None, None], 0), axis=0
    )
    filled = jnp.any(slot_match, axis=0)
    outgoing = jnp.where(
        filled[:, :, None], jnp.take(normed_full, source_rows, axis=0), jnp.zeros((), jnp.bfloat16)
    )
    arrived_rows = lax.all_to_all(outgoing, "expert", split_axis=0, concat_axis=0, tiled=True)
    flat_rows = arrived_rows.reshape(-1, arrived_rows.shape[-1])
    gate_val = jnp.dot(flat_rows, w_gate[0], preferred_element_type=jnp.float32)
    up_val = jnp.dot(flat_rows, w_up[0], preferred_element_type=jnp.float32)
    inner = (jax.nn.silu(gate_val) * up_val).astype(jnp.bfloat16)
    result = jnp.dot(inner, w_down[0], preferred_element_type=jnp.float32).astype(jnp.bfloat16)
    computed = result.reshape(arrived_rows.shape)
    returned = lax.all_to_all(computed, "expert", split_axis=0, concat_axis=0, tiled=True)
    combine_weights = jnp.where(slot_match, weight_slot[:, :, None], 0.0).astype(jnp.bfloat16)
    expert_part = jnp.einsum(
        "njc,jcd->nd", combine_weights, returned, preferred_element_type=jnp.float32
    )
    expert_share = lax.psum_scatter(
        expert_part.astype(jnp.bfloat16), "tensor", scatter_dimension=0, tiled=True
    ).astype(jnp.float32)
    return (hidden_state.astype(jnp.float32) + expert_share).astype(jnp.bfloat16)


def solution(mesh):
    return jax.shard_map(
        shards,
        mesh=mesh,
        in_specs=(
            P("expert", "tensor"),
            P("expert", None, None, None),
            P("expert"),
            P("tensor", "expert"),
            P(("expert", "tensor"), None),
            P(),
            P("expert", None),
            P("expert", None),
            P(("expert", "tensor"), None, None),
            P(("expert", "tensor"), None, None),
            P(("expert", "tensor"), None, None),
        ),
        out_specs=P(("expert", "tensor"), None),
        check_vma=False,
    )
```

profile of v0, /device:TPU:2, one launch (start us, length us, event | category | flops | bytes accessed | tf_op | source)
XLA Modules:
  0.0 520.2 jit_solution(15658658182001831944)
XLA Ops:
  6.5 0.0 copy-start
  6.5 0.0 all-gather.5.cloned.1.call-start
  6.5 0.7 all-gather.5.cloned.1.call-update
  7.3 0.0 all-gather.3.cloned.1.call-start
  7.3 0.7 all-gather.3.cloned.1.call-update
  8.0 0.0 all-reduce.2.cloned.1.call-start
  8.1 0.8 convert_reduce_fusion
  8.9 0.1 copy.36
  9.7 1.1 copy.38
  10.7 1.9 reduce_window_sum.14
  12.7 2.0 dynamic-slice_bitcast_fusion
  14.7 1.0 fusion.26
  15.7 5.1 fusion.62
  20.8 2.4 fusion.33
  23.2 51.8 %all-gather.5.cloned.1.call-done = bf16[512,4096]{1,0:T(8,128)(2,1)} async-done(((bf16[512,256]{1,0:T(8,128)(2,1)}), bf16[512,4096]{1,0:T(8,128)(2,1)}) %all-gather.5.cloned.1.call-update) | async-done | bytes 4194320 | tf_op jit(solution)/shard_map/all_gather | solution.py:87
  75.0 4.8 convolution_convert_fusion.1
  79.8 0.0 all-reduce.2.cloned.1.call-update
  79.8 0.9 fusion.57
  80.8 0.4 select_reduce_fusion
  81.2 0.1 reshape.155
  81.2 0.4 fusion.37
  81.6 34.7 %all-gather.3.cloned.1.call-done = bf16[256,4096]{1,0:T(8,128)(2,1)} async-done(((bf16[16,4096]{1,0:T(8,128)(2,1)}), bf16[256,4096]{1,0:T(8,128)(2,1)}) %all-gather.3.cloned.1.call-update) | async-done | bytes 2097168 | tf_op jit(solution)/shard_map/all_gather | solution.py:106
  116.4 115.7 %all-reduce.2.cloned.1.call-done = bf16[256,4096]{1,0:T(8,128)(2,1)} async-done(((bf16[256,4096]{1,0:T(8,128)(2,1)}), bf16[256,4096]{1,0:T(8,128)(2,1)}) %all-reduce.2.cloned.1.call-update) | async-done | bytes 2097168 | tf_op jit(solution)/shard_map/psum | solution.py:105
  232.1 3.2 fusion.6
  235.2 0.0 copy-start.1
  235.3 1.3 copy-done.1
  236.6 0.0 copy-done.3
  236.6 2.0 fusion.8
  238.6 13.8 %gather_fusion = bf16[768,4096]{1,0:T(8,128)(2,1)} fusion(bf16[256,4096]{1,0:T(8,128)(2,1)} %fusion.8, s32[1024]{0:T(1024)S(1)} %pad_clamp_fusion), kind=kCustom, calls=%fused_computation | custom fusion | bytes 12585984 | tf_op jit(solution)/shard_map/jit(_take)/gather | solution.py:115
  252.4 3.9 select_select_fusion
  256.3 0.0 copy-start.5
  256.3 79.0 %all_to_all.10 = bf16[16,48,4096]{2,1,0:T(8,128)(2,1)S(1)} all-to-all(bf16[16,48,4096]{2,1,0:T(8,128)(2,1)S(1)} %select_select_fusion), channel_id=1, replica_groups=mesh['expert'=16,'tensor'=16] {'expert'}, dimensions={0} | all-to-all | bytes 12582912 | tf_op jit(solution)/shard_map/all_to_all | solution.py:117
  335.3 0.0 copy-done.5
  335.3 3.4 fusion.12
  338.7 0.0 copy-done.6
  338.7 3.5 fusion.22
  342.2 0.0 copy-done
  342.2 5.4 %convolution_convert_fusion = bf16[768,4096]{1,0:T(8,128)(2,1)} fusion(bf16[768,384]{1,0:T(8,128)(2,1)S(1)} %fusion.22, bf16[1,384,4096]{2,1,0:T(8,128)(2,1)S(1)} %copy-done), kind=kOutput, calls=%fused_computation.2 | convolution fusion | flops 2419064832 | bytes 10027008 | tf_op jit(solution)/shard_map/dot_general | solution.py:122
  347.6 6.0 %all-to-all-start.1 = ((bf16[16,48,4096]{2,1,0:T(8,128)(2,1)}), bf16[16,48,4096]{2,1,0:T(8,128)(2,1)}, u32[]{:S(2)}, u32[]{:S(2)}) async-start(bf16[16,48,4096]{2,1,0:T(8,128)(2,1)} %bitcast.108), calls=%async_computation.1 | async-start | bytes 12582912 | tf_op jit(solution)/shard_map/all_to_all | solution.py:124
  353.6 0.0 reduce-scatter.2.cloned.1.call-start
  353.6 0.0 copy-done.4
  353.7 0.0 copy-done.2
  353.7 0.1 select_reduce_fusion.1
  353.8 87.2 %all-to-all-done.1 = bf16[16,48,4096]{2,1,0:T(8,128)(2,1)} async-done(((bf16[16,48,4096]{2,1,0:T(8,128)(2,1)}), bf16[16,48,4096]{2,1,0:T(8,128)(2,1)}, u32[]{:S(2)}, u32[]{:S(2)}) %all-to-all-start.1) | async-done | bytes 6291488 | tf_op jit(solution)/shard_map/all_to_all | solution.py:124
  441.0 6.0 %fusion.3 = bf16[256,4096]{1,0:T(8,128)(2,1)} fusion(bf16[16,48,4096]{2,1,0:T(8,128)(2,1)} %all-to-all-done.1, bf16[256,16]{0,1:T(8,128)(2,1)S(1)} %bitcast.119, s32[256,16]{0,1:T(8,128)S(1)} %bitcast.113, pred[256,16]{0,1:T(8,128)(4,1)S(1)} %bitcast.118), kind=kOutput, calls=%fused_computation.11 | convolution fusion | flops 1612251136 | bytes 8417280 | tf_op jit(solution)/shard_map/njc,jcd->nd/dot_general | solution.py:126
  447.0 0.0 reduce-scatter.2.cloned.1.call-update
  447.0 65.0 %reduce-scatter.2.cloned.1.call-done = bf16[16,4096]{1,0:T(8,128)(2,1)} async-done(((bf16[256,4096]{1,0:T(8,128)(2,1)}), bf16[16,4096]{1,0:T(8,128)(2,1)}) %reduce-scatter.2.cloned.1.call-update) | async-done | bytes 131088 | tf_op jit(solution)/shard_map/reduce_scatter | solution.py:129
  512.0 1.7 add_convert_fusion.1
  (20 shorter events, 0.2 us)
Async XLA Ops:
  6.5 335.7 %copy-start = (bf16[1,384,4096]{2,1,0:T(8,128)(2,1)S(1)}, bf16[1,384,4096]{2,1,0:T(8,128)(2,1)}, u32[]{:S(2)}) copy-start(bf16[1,384,4096]{2,1,0:T(8,128)(2,1)} %param.21) | copy-start | bytes 9437188
  6.5 68.5 %all-gather.5.cloned.1.call-start = ((), (), s32[]{:S(2)}) async-start(), calls=%async_computation.4 | async-start | bytes 4456448 | tf_op jit(solution)/shard_map/all_gather | solution.py:87
  7.3 109.1 %all-gather.3.cloned.1.call-start = ((), (), s32[]{:S(2)}) async-start(), calls=%async_computation.3 | async-start | bytes 2228224 | tf_op jit(solution)/shard_map/all_gather | solution.py:106
  8.0 224.1 %all-reduce.2.cloned.1.call-start = ((), (), s32[]{:S(2)}) async-start(), calls=%async_computation.5 | async-start | bytes 4194304 | tf_op jit(solution)/shard_map/psum | solution.py:105
  79.8 156.8 %copy-start.3 = (f32[4096]{0:T(1024)S(1)}, f32[4096]{0:T(1024)}, u32[]{:S(2)}) copy-start(f32[4096]{0:T(1024)} %param.16) | copy-start | bytes 49156
  235.2 1.4 copy-start.1
  256.3 79.0 %copy-start.5 = (bf16[1,4096,384]{2,1,0:T(8,128)(2,1)S(1)}, bf16[1,4096,384]{2,1,0:T(8,128)(2,1)}, u32[]{:S(2)}) copy-start(bf16[1,4096,384]{2,1,0:T(8,128)(2,1)} %param.19) | copy-start | bytes 9437188
  335.3 3.4 copy-start.6
  347.6 6.0 %copy-start.4 = (bf16[256,8]{0,1:T(8,128)(2,1)S(1)}, bf16[256,8]{0,1:T(8,128)(2,1)}, u32[]{:S(2)}) copy-start(bf16[256,8]{0,1:T(8,128)(2,1)} %param.18) | copy-start | bytes 12292
  347.6 6.0 %copy-start.2 = (s32[256,8]{0,1:T(8,128)S(1)}, s32[256,8]{0,1:T(8,128)}, u32[]{:S(2)}) copy-start(s32[256,8]{0,1:T(8,128)} %param.17) | copy-start | bytes 24580
  347.6 93.4 %all-to-all-start.1 = ((bf16[16,48,4096]{2,1,0:T(8,128)(2,1)}), bf16[16,48,4096]{2,1,0:T(8,128)(2,1)}, u32[]{:S(2)}, u32[]{:S(2)}) async-start(bf16[16,48,4096]{2,1,0:T(8,128)(2,1)} %bitcast.108), calls=%async_computation.1 | async-start | bytes 12582912 | tf_op jit(solution)/shard_map/all_to_all | solution.py:124
  353.6 158.4 %reduce-scatter.2.cloned.1.call-start = ((), (), s32[]{:S(2)}) async-start(), calls=%async_computation.6 | async-start | bytes 2228224 | tf_op jit(solution)/shard_map/reduce_scatter | solution.py:129
Sparse Core Ops, SparseCore 0:
  9.8 65.2 all-gather.4
  76.8 39.4 all-gather.2
  118.7 113.3 all-reduce.1
  447.2 64.7 reduce-scatter.1
where the time goes:
time: 521 us; the launch traced here: 520 us
  waiting for transfers between devices  356 us (68%)
  blocking collectives  79 us (15%)
  matrix products  30.6 us (6%)
  local copies, waits for them, and re-layouts  20.5 us (4%)
  other arithmetic  14.3 us (3%)
  between operations  14 us (3%)
  starting transfers between devices  6.07 us (1%)
    psum x1, waiting for transfers between devices, shards(): lax.psum(head_part.astype(jnp.bfloat16), 'tensor').astype(jnp.float32)  116 us
    all_to_all x1, waiting for transfers between devices, shards(): lax.all_to_all(computed, 'expert', split_axis=0, concat_axis=0, tiled=True)  87.2 us
    all_to_all x1, blocking collectives, shards(): lax.all_to_all(outgoing, 'expert', split_axis=0, concat_axis=0, tiled=True)  79 us
    reduce_scatter x1, waiting for transfers between devices, shards(): lax.psum_scatter(expert_part.astype(jnp.bfloat16), 'tensor', scatter_dime...  65 us
    all_gather x1, waiting for transfers between devices, shards(): lax.all_gather(out_proj, 'expert', axis=1, tiled=True)  51.8 us
    all_gather x1, waiting for transfers between devices, shards(): residual_full = lax.all_gather(residual, 'tensor', axis=0, tiled=True)  34.7 us
    gather x1, local copies, waits for them, and re-layouts, shards(): jnp.take(normed_full, source_rows, axis=0)  13.8 us
  transfers between devices with their start and end apart: 5, of which 5 were waited for; matrix products, arithmetic and copies ran while one was open for 4% of the time, Pallas kernels for 0%

commit v1 on v0

--- a/solution.py
+++ b/solution.py
@@ -84,7 +84,9 @@
     )
     head_part = jnp.dot(
         attended,
-        lax.all_gather(out_proj, "expert", axis=1, tiled=True),
+        jnp.concatenate(
+            lax.all_to_all(jnp.stack([out_proj] * lax.axis_size("expert")), "expert", 0, 0), axis=1
+        ),
         preferred_element_type=jnp.float32,
     )
     slot_count = tensor_count // HSPLIT

time: 521 us -> 490 us (0.940)
  waiting for transfers between devices: 356 us -> 314 us
  starting transfers between devices: 6.07 us -> 13.7 us
    all_gather x1 -> x0, waiting for transfers between devices: 51.8 us -> none  [shards(): lax.all_gather(out_proj, 'expert', axis=1, tiled=True)]
    all_to_all x0 -> x1, waiting for transfers between devices: none -> 43.7 us  [shards(): lax.all_to_all(jnp.stack([out_proj] * lax.axis_size('expert')), 'expert',...]
    all_gather x1, waiting for transfers between devices: 34.7 us -> 0.02 us  [shards(): residual_full = lax.all_gather(residual, 'tensor', axis=0, tiled=True)]
    all_to_all x0 -> x1, starting transfers between devices: none -> 7.61 us  [shards(): lax.all_to_all(jnp.stack([out_proj] * lax.axis_size('expert')), 'expert',...]
  transfers between devices with their start and end apart: 5 -> 5, of which waited for: 5 -> 4; matrix products, arithmetic and copies ran while one was open for 4% -> 4% of each run, Pallas kernels for 0% -> 0%
where the time goes in v1:
time: 490 us; the launch traced here: 489 us
  waiting for transfers between devices  314 us (64%)
  blocking collectives  79 us (16%)
  matrix products  30.7 us (6%)
  local copies, waits for them, and re-layouts  24.1 us (5%)
  between operations  14 us (3%)
  starting transfers between devices  13.7 us (3%)
  other arithmetic  13.6 us (3%)
    psum x1, waiting for transfers between devices, shards(): lax.psum(head_part.astype(jnp.bfloat16), 'tensor').astype(jnp.float32)  118 us
    all_to_all x1, waiting for transfers between devices, shards(): lax.all_to_all(computed, 'expert', split_axis=0, concat_axis=0, tiled=True)  87.2 us
    all_to_all x1, blocking collectives, shards(): lax.all_to_all(outgoing, 'expert', split_axis=0, concat_axis=0, tiled=True)  79 us
    reduce_scatter x1, waiting for transfers between devices, shards(): lax.psum_scatter(expert_part.astype(jnp.bfloat16), 'tensor', scatter_dime...  64.9 us
    all_to_all x1, waiting for transfers between devices, shards(): lax.all_to_all(jnp.stack([out_proj] * lax.axis_size('expert')), 'expert',...  43.7 us
    gather x1, local copies, waits for them, and re-layouts, shards(): jnp.take(normed_full, source_rows, axis=0)  13.8 us
  transfers between devices with their start and end apart: 5, of which 4 were waited for; matrix products, arithmetic and copies ran while one was open for 4% of the time, Pallas kernels for 0%

profile of v1, /device:TPU:2, one launch (start us, length us, event | category | flops | bytes accessed | tf_op | source)
XLA Modules:
  0.0 489.2 jit_solution(16437509157023381475)
XLA Ops:
  6.5 0.0 copy-start
  6.5 1.2 copy.38
  7.8 2.4 stack.2
  10.2 7.6 %all-to-all-start = ((bf16[16,512,256]{1,2,0:T(8,128)(2,1)}), bf16[16,512,256]{1,2,0:T(8,128)(2,1)}, u32[]{:S(2)}, u32[]{:S(2)}) async-start(bf16[16,512,256]{1,2,0:T(8,128)(2,1)} %stack.2), calls=%async_computation | async-start | bytes 8388608 | tf_op jit(solution)/shard_map/all_to_all | solution.py:88
  17.8 0.0 all-gather.2.cloned.1.call-start
  17.8 0.7 all-gather.2.cloned.1.call-update
  18.5 0.0 all-reduce.2.cloned.1.call-start
  18.6 0.0 copy-done.2
  18.6 0.1 convert_reduce_fusion
  18.7 0.1 copy.39
  19.5 1.1 copy.41
  20.6 1.9 reduce_window_sum.14
  22.5 2.0 dynamic-slice_bitcast_fusion
  24.6 1.0 fusion.26
  25.6 5.2 %fusion.62 = (f32[4,256]{1,0:T(4,128)S(1)}, bf16[4,256,1280]{1,2,0:T(8,128)(2,1)}) fusion(pred[256,1280]{0,1:T(8,128)(4,1)S(1)} %fusion.26, bf16[1280,256]{1,0:T(8,128)(2,1)} %dynamic-slice_bitcast_fusion, bf16[256,512]{1,0:T(8,128)(2,1)} %param.11), kind=kOutput, calls=%fused_computation.84 | convolution fusion | flops 680264960 | bytes 4460544 | tf_op jit(solution)/shard_map/sub | solution.py:75
  30.8 2.4 fusion.33
  33.2 43.7 %all-to-all-done = bf16[16,512,256]{1,2,0:T(8,128)(2,1)} async-done(((bf16[16,512,256]{1,2,0:T(8,128)(2,1)}), bf16[16,512,256]{1,2,0:T(8,128)(2,1)}, u32[]{:S(2)}, u32[]{:S(2)}) %all-to-all-start) | async-done | bytes 4194336 | tf_op jit(solution)/shard_map/all_to_all | solution.py:88
  76.8 4.8 convolution_convert_fusion.1
  81.7 0.0 all-reduce.2.cloned.1.call-update
  81.7 0.9 fusion.57
  82.6 0.4 select_reduce_fusion
  83.0 0.1 reshape.165
  83.1 0.4 fusion.37
  83.5 0.0 all-gather.2.cloned.1.call-done
  83.5 117.6 %all-reduce.2.cloned.1.call-done = bf16[256,4096]{1,0:T(8,128)(2,1)} async-done(((bf16[256,4096]{1,0:T(8,128)(2,1)}), bf16[256,4096]{1,0:T(8,128)(2,1)}) %all-reduce.2.cloned.1.call-update) | async-done | bytes 2097168 | tf_op jit(solution)/shard_map/psum | solution.py:107
  201.1 3.2 fusion.6
  204.3 0.0 copy-start.1
  204.3 1.3 copy-done.1
  205.7 0.0 copy-done.3
  205.7 2.0 fusion.8
  207.7 13.8 %gather_fusion = bf16[768,4096]{1,0:T(8,128)(2,1)} fusion(bf16[256,4096]{1,0:T(8,128)(2,1)} %fusion.8, s32[1024]{0:T(1024)S(1)} %pad_clamp_fusion), kind=kCustom, calls=%fused_computation | custom fusion | bytes 12585984 | tf_op jit(solution)/shard_map/jit(_take)/gather | solution.py:117
  221.5 3.9 select_select_fusion
  225.4 0.0 copy-start.5
  225.4 79.0 %all_to_all.15 = bf16[16,48,4096]{2,1,0:T(8,128)(2,1)S(1)} all-to-all(bf16[16,48,4096]{2,1,0:T(8,128)(2,1)S(1)} %select_select_fusion), channel_id=1, replica_groups=mesh['expert'=16,'tensor'=16] {'expert'}, dimensions={0} | all-to-all | bytes 12582912 | tf_op jit(solution)/shard_map/all_to_all | solution.py:119
  304.4 0.0 copy-done.5
  304.4 3.4 fusion.12
  307.8 0.0 copy-done.6
  307.8 3.5 fusion.22
  311.3 0.0 copy-done
  311.3 5.4 %convolution_convert_fusion = bf16[768,4096]{1,0:T(8,128)(2,1)} fusion(bf16[768,384]{1,0:T(8,128)(2,1)S(1)} %fusion.22, bf16[1,384,4096]{2,1,0:T(8,128)(2,1)S(1)} %copy-done), kind=kOutput, calls=%fused_computation.2 | convolution fusion | flops 2419064832 | bytes 10027008 | tf_op jit(solution)/shard_map/dot_general | solution.py:124
  316.7 6.0 %all-to-all-start.2 = ((bf16[16,48,4096]{2,1,0:T(8,128)(2,1)}), bf16[16,48,4096]{2,1,0:T(8,128)(2,1)}, u32[]{:S(2)}, u32[]{:S(2)}) async-start(bf16[16,48,4096]{2,1,0:T(8,128)(2,1)} %bitcast.111), calls=%async_computation.2 | async-start | bytes 12582912 | tf_op jit(solution)/shard_map/all_to_all | solution.py:126
  322.7 0.0 reduce-scatter.2.cloned.1.call-start
  322.7 0.1 select_reduce_fusion.1
  322.9 87.2 %all-to-all-done.2 = bf16[16,48,4096]{2,1,0:T(8,128)(2,1)} async-done(((bf16[16,48,4096]{2,1,0:T(8,128)(2,1)}), bf16[16,48,4096]{2,1,0:T(8,128)(2,1)}, u32[]{:S(2)}, u32[]{:S(2)}) %all-to-all-start.2) | async-done | bytes 6291488 | tf_op jit(solution)/shard_map/all_to_all | solution.py:126
  410.1 6.0 %fusion.3 = bf16[256,4096]{1,0:T(8,128)(2,1)} fusion(bf16[16,48,4096]{2,1,0:T(8,128)(2,1)} %all-to-all-done.2, bf16[256,16]{0,1:T(8,128)(2,1)S(1)} %bitcast.122, s32[256,16]{0,1:T(8,128)S(1)} %bitcast.116, pred[256,16]{0,1:T(8,128)(4,1)S(1)} %bitcast.121), kind=kOutput, calls=%fused_computation.11 | convolution fusion | flops 1612251136 | bytes 8417280 | tf_op jit(solution)/shard_map/njc,jcd->nd/dot_general | solution.py:128
  416.1 0.0 reduce-scatter.2.cloned.1.call-update
  416.1 64.9 %reduce-scatter.2.cloned.1.call-done = bf16[16,4096]{1,0:T(8,128)(2,1)} async-done(((bf16[256,4096]{1,0:T(8,128)(2,1)}), bf16[16,4096]{1,0:T(8,128)(2,1)}) %reduce-scatter.2.cloned.1.call-update) | async-done | bytes 131088 | tf_op jit(solution)/shard_map/reduce_scatter | solution.py:131
  481.0 1.7 add_convert_fusion.1
  (21 shorter events, 0.2 us)
Async XLA Ops:
  6.5 304.7 %copy-start = (bf16[1,384,4096]{2,1,0:T(8,128)(2,1)S(1)}, bf16[1,384,4096]{2,1,0:T(8,128)(2,1)}, u32[]{:S(2)}) copy-start(bf16[1,384,4096]{2,1,0:T(8,128)(2,1)} %param.21) | copy-start | bytes 9437188
  10.2 8.4 %copy-start.2 = (s32[256,8]{0,1:T(8,128)S(1)}, s32[256,8]{0,1:T(8,128)}, u32[]{:S(2)}) copy-start(s32[256,8]{0,1:T(8,128)} %param.17) | copy-start | bytes 24580
  10.2 66.7 %all-to-all-start = ((bf16[16,512,256]{1,2,0:T(8,128)(2,1)}), bf16[16,512,256]{1,2,0:T(8,128)(2,1)}, u32[]{:S(2)}, u32[]{:S(2)}) async-start(bf16[16,512,256]{1,2,0:T(8,128)(2,1)} %stack.2), calls=%async_computation | async-start | bytes 8388608 | tf_op jit(solution)/shard_map/all_to_all | solution.py:88
  17.8 65.7 %all-gather.2.cloned.1.call-start = ((), (), s32[]{:S(2)}) async-start(), calls=%async_computation.4 | async-start | bytes 2228224 | tf_op jit(solution)/shard_map/all_gather | solution.py:108
  18.5 182.6 %all-reduce.2.cloned.1.call-start = ((), (), s32[]{:S(2)}) async-start(), calls=%async_computation.5 | async-start | bytes 4194304 | tf_op jit(solution)/shard_map/psum | solution.py:107
  81.7 124.0 %copy-start.3 = (f32[4096]{0:T(1024)S(1)}, f32[4096]{0:T(1024)}, u32[]{:S(2)}) copy-start(f32[4096]{0:T(1024)} %param.16) | copy-start | bytes 49156
  204.3 1.4 copy-start.1
  225.4 79.0 %copy-start.5 = (bf16[1,4096,384]{2,1,0:T(8,128)(2,1)S(1)}, bf16[1,4096,384]{2,1,0:T(8,128)(2,1)}, u32[]{:S(2)}) copy-start(bf16[1,4096,384]{2,1,0:T(8,128)(2,1)} %param.19) | copy-start | bytes 9437188
  304.4 3.4 copy-start.6
  316.7 6.0 %copy-start.4 = (bf16[256,8]{0,1:T(8,128)(2,1)S(1)}, bf16[256,8]{0,1:T(8,128)(2,1)}, u32[]{:S(2)}) copy-start(bf16[256,8]{0,1:T(8,128)(2,1)} %param.18) | copy-start | bytes 12292
  316.7 93.4 %all-to-all-start.2 = ((bf16[16,48,4096]{2,1,0:T(8,128)(2,1)}), bf16[16,48,4096]{2,1,0:T(8,128)(2,1)}, u32[]{:S(2)}, u32[]{:S(2)}) async-start(bf16[16,48,4096]{2,1,0:T(8,128)(2,1)} %bitcast.111), calls=%async_computation.2 | async-start | bytes 12582912 | tf_op jit(solution)/shard_map/all_to_all | solution.py:126
  322.7 158.4 %reduce-scatter.2.cloned.1.call-start = ((), (), s32[]{:S(2)}) async-start(), calls=%async_computation.6 | async-start | bytes 2228224 | tf_op jit(solution)/shard_map/reduce_scatter | solution.py:131
Sparse Core Ops, SparseCore 0:
  20.4 42.4 all-gather.1
  81.8 119.2 all-reduce.1
  416.2 64.7 reduce-scatter.1
